TPU v7x, 256 devices: a whole 4x4x8 slice. The times are simulated.
256 devices in a mesh: seq: 64 (over z_lo, x, y), batch: 4 (over z_hi, core).
Axes of the slice: x: 4, y: 4, z: 8 (z_hi: 2, z_lo: 4; z = z_hi * 4 + z_lo), core: 2. Of those that a mesh axis runs over, the one named last changes fastest.
Arguments:
- inputs: bfloat16 [4, 16384, 2048], P('batch', 'seq'), may hold values from -106.50967 to 106.50967
- output_grad: bfloat16 [4, 16384, 2048], P('batch', 'seq'), may hold values from -6 to 6
- norm_gain: float32 [2048], replicated, may hold values from 0.1 to 1.9
- gate_bias: float32 [2048], P('seq'), as said below
- state_in: float32 [4, 2048], P('batch', 'seq'), may hold values from -6 to 6
- w_gate: bfloat16 [2048, 2048], P('seq'), may hold values from -0.44194174 to 0.44194174
- w_cand: bfloat16 [2048, 2048], P('seq'), may hold values from -0.125 to 0.125
- w_out: bfloat16 [2048, 2048], P('seq'), may hold values from -0.125 to 0.125
Outputs:
- layer_out: bfloat16 [4, 16384, 2048], P('batch', 'seq')
- input_grad: bfloat16 [4, 16384, 2048], P('batch', 'seq')
- state_grad: float32 [4, 2048], P('batch', 'seq')
- bias_grad: float32 [2048], P('seq')
Inputs may be any that keep to these rules, and one draw needn't show every extreme that they name: `gate_bias`: every value is at least -ln(16384) - 1.5.
All inputs are finite; a program needn't handle non-finite values.
Results may differ from a plain program's by a relative error of at most 0.013.
Values may be sent and summed in bfloat16 or wider, within the bound.
A program may use at most 128 MiB of HBM per device.

v0:
```python
import jax
import jax.numpy as jnp
from jax import lax
from jax.sharding import PartitionSpec as P

EPSILON = 1e-06


def shifted(values, axis, offset, fill, reverse):
    length = values.shape[axis]
    pad_shape = list(values.shape)
    pad_shape[axis] = offset
    padding = jnp.full(tuple(pad_shape), fill, values.dtype)
    if reverse:
        kept = lax.slice_in_dim(values, offset, length, 1, axis)
        return jnp.concatenate([kept, padding], axis=axis)
    kept = lax.slice_in_dim(values, 0, length - offset, 1, axis)
    return jnp.concatenate([padding, kept], axis=axis)


def shift_scan(keep, drive, axis, reverse):
    length = keep.shape[axis]
    offset = 1
    while offset < length:
        keep_far = shifted(keep, axis, offset, 1.0, reverse)
        drive_far = shifted(drive, axis, offset, 0.0, reverse)
        drive = keep * drive_far + drive
        keep = keep * keep_far
        offset = offset * 2
    return (keep, drive)


def on_device(inputs, output_grad, norm_gain, gate_bias, state_in, w_gate, w_cand, w_out):
    token_rows = inputs[0]
    grad_rows = output_grad[0]
    gate_full, cand_full, out_full = (
        lax.all_gather(w_gate, "seq", axis=0, tiled=True),
        lax.all_gather(w_cand, "seq", axis=0, tiled=True),
        lax.all_gather(w_out, "seq", axis=0, tiled=True),
    )
    residual = token_rows.astype(jnp.float32)
    mean_square = jnp.mean(residual * residual, axis=-1, keepdims=True)
    inverse_rms = lax.rsqrt(mean_square + EPSILON)
    unit_rows = residual * inverse_rms
    normed = (unit_rows * norm_gain).astype(jnp.bfloat16)
    hidden_dim = 0
    contract_model = (((0,), (1,)), ((), ()))
    gate_pre = lax.dot_general(
        gate_full, normed, contract_model, preferred_element_type=jnp.float32
    ).astype(jnp.bfloat16)
    cand_pre = lax.dot_general(
        cand_full, normed, contract_model, preferred_element_type=jnp.float32
    ).astype(jnp.bfloat16)
    back_grads = lax.dot_general(
        out_full, grad_rows, (((1,), (1,)), ((), ())), preferred_element_type=jnp.float32
    ).astype(jnp.bfloat16)
    gate_slab, cand_slab = (
        lax.all_to_all(gate_pre, "seq", split_axis=0, concat_axis=1, tiled=True),
        lax.all_to_all(cand_pre, "seq", split_axis=0, concat_axis=1, tiled=True),
    )
    gate_input = gate_slab.astype(jnp.float32) + gate_bias[:, None]
    update = jax.nn.sigmoid(gate_input)
    retain = jax.nn.sigmoid(-gate_input)
    candidate = cand_slab.astype(jnp.float32)
    initial = state_in[0]
    drive_term = (update * candidate).at[:, 0].add(retain[:, 0] * initial)
    reached, states = shift_scan(retain, drive_term, 1, False)
    state_tok = lax.all_to_all(
        states.astype(jnp.bfloat16), "seq", split_axis=1, concat_axis=0, tiled=True
    )
    back_slab = lax.all_to_all(back_grads, "seq", split_axis=0, concat_axis=1, tiled=True)
    next_retain = jnp.concatenate(
        [retain[:, 1:], jnp.zeros((retain.shape[0], 1), jnp.float32)], axis=1
    )
    tail_keep, carried = shift_scan(next_retain, back_slab.astype(jnp.float32), 1, True)
    state_grad = retain[:, 0] * carried[:, 0]
    earlier_states = jnp.concatenate([initial[:, None], states[:, :-1]], axis=1)
    gate_grad = carried * (candidate - earlier_states) * update * retain
    cand_grad = carried * update
    bias_part = jnp.sum(gate_grad, axis=1)
    gate_tok, cand_tok = (
        lax.all_to_all(
            gate_grad.astype(jnp.bfloat16), "seq", split_axis=1, concat_axis=0, tiled=True
        ),
        lax.all_to_all(
            cand_grad.astype(jnp.bfloat16), "seq", split_axis=1, concat_axis=0, tiled=True
        ),
    )
    contract_hidden = (((hidden_dim,), (0,)), ((), ()))
    layer_rows = (
        residual
        + lax.dot_general(state_tok, out_full, contract_hidden, preferred_element_type=jnp.float32)
    ).astype(jnp.bfloat16)
    contract_back = (((hidden_dim,), (1,)), ((), ()))
    normed_grad = lax.dot_general(
        gate_tok, gate_full, contract_back, preferred_element_type=jnp.float32
    )
    normed_grad = normed_grad + lax.dot_general(
        cand_tok, cand_full, contract_back, preferred_element_type=jnp.float32
    )
    unit_grad = normed_grad * norm_gain
    input_rows = inverse_rms * (
        unit_grad - unit_rows * jnp.mean(unit_grad * unit_rows, axis=-1, keepdims=True)
    )
    token_grad = (grad_rows.astype(jnp.float32) + input_rows).astype(jnp.bfloat16)
    bias_grad = lax.psum(bias_part, "batch")
    return (layer_rows[None], token_grad[None], state_grad[None], bias_grad)


def solution(mesh):
    return jax.shard_map(
        on_device,
        mesh=mesh,
        in_specs=(
            P("batch", "seq", None),
            P("batch", "seq", None),
            P(),
            P("seq"),
            P("batch", "seq"),
            P("seq", None),
            P("seq", None),
            P("seq", None),
        ),
        out_specs=(P("batch", "seq", None), P("batch", "seq", None), P("batch", "seq"), P("seq")),
        check_vma=False,
    )
```

profile of v0, /device:TPU:8, one launch (start us, length us, event | category | flops | bytes accessed | tf_op | source)
XLA Modules:
  0.0 1306.1 jit_solution(2977227251477616313)
XLA Ops:
  10.9 361.7 %all-gather.6.cloned.1.call-done = bf16[2048,2048]{1,0:T(8,128)(2,1)} async-done(((bf16[32,2048]{1,0:T(8,128)(2,1)}), bf16[2048,2048]{1,0:T(8,128)(2,1)}) %all-gather.6.cloned.1.call-update) | async-done | bytes 8388624 | tf_op jit(solution)/shard_map/all_gather | solution.py:38
  372.6 6.1 fusion.6
  380.0 10.6 all-to-all-start.1
  390.6 343.9 %all-gather.4.cloned.1.call-done = bf16[2048,2048]{1,0:T(8,128)(2,1)} async-done(((bf16[32,2048]{1,0:T(8,128)(2,1)}), bf16[2048,2048]{1,0:T(8,128)(2,1)}) %all-gather.4.cloned.1.call-update) | async-done | bytes 8388624 | tf_op jit(solution)/shard_map/all_gather | solution.py:37
  734.5 6.7 fusion.5
  741.2 2.3 copy.31
  743.6 9.9 all-to-all-start
  753.5 340.4 %all-gather.8.cloned.1.call-done = bf16[2048,2048]{1,0:T(8,128)(2,1)} async-done(((bf16[32,2048]{1,0:T(8,128)(2,1)}), bf16[2048,2048]{1,0:T(8,128)(2,1)}) %all-gather.8.cloned.1.call-update) | async-done | bytes 8388624 | tf_op jit(solution)/shard_map/all_gather | solution.py:39
  1093.9 6.7 convolution_convert_fusion
  1100.6 11.7 all-to-all-start.3
  1113.3 1.6 copy.45
  1116.7 13.5 %all-to-all-done.3 = bf16[64,32,256]{2,1,0:T(8,128)(2,1)} async-done(((bf16[64,32,256]{2,1,0:T(8,128)(2,1)}), bf16[64,32,256]{2,1,0:T(8,128)(2,1)}, u32[]{:S(2)}, u32[]{:S(2)}) %all-to-all-start.3) | async-done | bytes 1048608 | tf_op jit(solution)/shard_map/all_to_all | solution.py:71
  1131.9 2.0 slice.294
  1136.8 2.6 fusion.27
  1141.4 4.3 multiply_add_fusion.27
  1148.3 2.5 slice_multiply_fusion
  1151.8 2.1 slice.296
  1153.9 10.3 multiply_add_fusion.11
  1164.2 4.6 multiply_add_fusion.25
  1173.6 9.4 multiply_add_fusion.20
  1202.8 2.9 fusion.24
  1206.8 6.2 all-to-all-start.4
  1213.0 2.8 multiply_convert_fusion
  1217.0 14.3 %all-to-all-done.4 = bf16[32,64,256]{2,0,1:T(8,128)(2,1)} async-done(((bf16[32,64,256]{2,0,1:T(8,128)(2,1)}), bf16[32,64,256]{2,0,1:T(8,128)(2,1)}, u32[]{:S(2)}, u32[]{:S(2)}) %all-to-all-start.4) | async-done | bytes 1048608 | tf_op jit(solution)/shard_map/all_to_all | solution.py:82
  1231.2 6.2 all-to-all-start.5
  1238.6 16.1 %psum.7 = f32[32]{0:T(128)} all-reduce(f32[32]{0:T(128)S(1)} %get-tuple-element.16), channel_id=1, replica_groups=mesh['seq'=64,'batch'=4] {'batch'}, use_global_device_ids=true, to_apply=%region_4.0 | all-reduce | flops 32 | bytes 256 | tf_op jit(solution)/shard_map/psum | solution.py:106
  1256.1 11.1 all-to-all-start.2
  1267.2 6.2 fusion.28
  1273.4 6.5 fusion.9
  1280.0 1.6 fusion.18
  1281.6 10.9 all-to-all-done.2
  1292.5 6.7 fusion.7
  (136 shorter events, 46.9 us)
Async XLA Ops:
  7.2 365.4 %all-gather.6.cloned.1.call-start = ((), (), s32[]{:S(2)}) async-start(), calls=%async_computation.7 | async-start | bytes 8519680 | tf_op jit(solution)/shard_map/all_gather | solution.py:38
  7.9 726.6 %all-gather.4.cloned.1.call-start = ((), (), s32[]{:S(2)}) async-start(), calls=%async_computation.6 | async-start | bytes 8519680 | tf_op jit(solution)/shard_map/all_gather | solution.py:37
  8.6 1085.2 %all-gather.8.cloned.1.call-start = ((), (), s32[]{:S(2)}) async-start(), calls=%async_computation.8 | async-start | bytes 8519680 | tf_op jit(solution)/shard_map/all_gather | solution.py:39
  10.9 723.6 %copy-start.20 = (f32[256]{0:T(256)}, f32[256]{0:T(256)S(1)}, u32[]{:S(2)}) copy-start(f32[256]{0:T(256)S(1)} %add_rsqrt_fusion) | copy-start | bytes 3076
  378.7 355.8 %copy-start.12 = (bf16[1,256,2048]{2,1,0:T(8,128)(2,1)S(1)}, bf16[1,256,2048]{2,1,0:T(8,128)(2,1)}, u32[]{:S(2)}) copy-start(bf16[1,256,2048]{2,1,0:T(8,128)(2,1)} %param.10) | copy-start | bytes 3145732
  378.7 355.8 %copy-start.23 = (f32[2048]{0:T(1024)S(1)}, f32[2048]{0:T(1024)}, u32[]{:S(2)}) copy-start(f32[2048]{0:T(1024)} %param.12) | copy-start | bytes 24580
  380.0 363.5 %all-to-all-start.1 = ((bf16[64,32,256]{2,1,0:T(8,128)(2,1)}), bf16[64,32,256]{2,1,0:T(8,128)(2,1)S(1)}, u32[]{:S(2)}, u32[]{:S(2)}) async-start(bf16[64,32,256]{2,1,0:T(8,128)(2,1)} %bitcast.6), calls=%async_computation.1 | async-start | bytes 2097152 | tf_op jit(solution)/shard_map/all_to_all | solution.py:59
  741.2 352.6 %copy-start.17 = (bf16[1,256,2048]{2,1,0:T(8,128)(2,1)S(1)}, bf16[1,256,2048]{2,1,0:T(8,128)(2,1)}, u32[]{:S(2)}) copy-start(bf16[1,256,2048]{2,1,0:T(8,128)(2,1)} %param.11) | copy-start | bytes 3145732
  743.6 357.0 %all-to-all-start = ((bf16[64,32,256]{2,1,0:T(8,128)(2,1)}), bf16[64,32,256]{2,1,0:T(8,128)(2,1)S(1)}, u32[]{:S(2)}, u32[]{:S(2)}) async-start(bf16[64,32,256]{2,1,0:T(8,128)(2,1)} %bitcast.3), calls=%async_computation | async-start | bytes 2097152 | tf_op jit(solution)/shard_map/all_to_all | solution.py:58
  1100.6 11.7 copy-start.22
  1100.6 11.8 copy-start.15
  1100.6 29.6 %all-to-all-start.3 = ((bf16[64,32,256]{2,1,0:T(8,128)(2,1)}), bf16[64,32,256]{2,1,0:T(8,128)(2,1)}, u32[]{:S(2)}, u32[]{:S(2)}) async-start(bf16[64,32,256]{2,1,0:T(8,128)(2,1)} %bitcast.110), calls=%async_computation.3 | async-start | bytes 2097152 | tf_op jit(solution)/shard_map/all_to_all | solution.py:71
  1113.3 1.6 copy-start.16
  1131.8 2.1 copy-start.5
  1131.9 3.1 copy-start.2
  1131.9 3.7 copy-start.8
  1131.9 3.7 copy-start.19
  1136.8 2.6 copy-start.4
  1141.4 4.3 copy-start
  1145.7 2.2 copy-start.14
  1147.9 3.5 copy-start.1
  1151.8 2.1 copy-start.7
  1186.4 1.6 copy-start.10
  1200.6 1.6 copy-start.3
  1200.6 2.2 copy-start.9
  1206.8 24.5 %all-to-all-start.4 = ((bf16[32,64,256]{2,0,1:T(8,128)(2,1)}), bf16[32,64,256]{2,0,1:T(8,128)(2,1)}, u32[]{:S(2)}, u32[]{:S(2)}) async-start(bf16[32,64,256]{2,0,1:T(8,128)(2,1)} %bitcast.107), calls=%async_computation.4 | async-start | bytes 2097152 | tf_op jit(solution)/shard_map/all_to_all | solution.py:82
  1231.2 24.8 %all-to-all-start.5 = ((bf16[32,64,256]{2,0,1:T(8,128)(2,1)}), bf16[32,64,256]{2,0,1:T(8,128)(2,1)}, u32[]{:S(2)}, u32[]{:S(2)}) async-start(bf16[32,64,256]{2,0,1:T(8,128)(2,1)} %bitcast.106), calls=%async_computation.5 | async-start | bytes 2097152 | tf_op jit(solution)/shard_map/all_to_all | solution.py:85
  1256.1 36.4 %all-to-all-start.2 = ((bf16[32,64,256]{2,0,1:T(8,128)(2,1)}), bf16[32,64,256]{2,0,1:T(8,128)(2,1)S(1)}, u32[]{:S(2)}, u32[]{:S(2)}) async-start(bf16[32,64,256]{2,0,1:T(8,128)(2,1)} %bitcast.105), calls=%async_computation.2 | async-start | bytes 2097152 | tf_op jit(solution)/shard_map/all_to_all | solution.py:68
  1267.2 6.2 copy-start.13
  1267.2 6.2 copy-start.21
  1267.2 6.2 copy-start.24
  1273.4 6.5 copy-start.18
  (2 other events, 3.2 us)
Sparse Core Ops, SparseCore 0:
  9.8 362.7 all-gather.5
  374.4 360.0 all-gather.3
  736.3 357.5 all-gather.7
where the time goes:
time: 1310 us
  waiting for transfers between devices  1090 us (83%)
  other arithmetic  57.8 us (4%)
  starting transfers between devices  55.8 us (4%)
  matrix products  39 us (3%)
  local copies, waits for them, and re-layouts  36 us (3%)
  blocking collectives  16.1 us (1%)
  between operations  14.9 us (1%)
    all_gather x1, waiting for transfers between devices, on_device(): lax.all_gather(w_cand, 'seq', axis=0, tiled=True)  362 us
    all_gather x1, waiting for transfers between devices, on_device(): lax.all_gather(w_gate, 'seq', axis=0, tiled=True)  344 us
    all_gather x1, waiting for transfers between devices, on_device(): lax.all_gather(w_out, 'seq', axis=0, tiled=True)  340 us
    add x25, other arithmetic, shift_scan(): drive = keep * drive_far + drive  40.3 us
  transfers between devices with their start and end apart: 9, of which 6 were waited for; matrix products, arithmetic and copies ran while one was open for 4% of the time, Pallas kernels for 0%

commit v1 on v0

--- a/solution.py
+++ b/solution.py
@@ -34,7 +34,9 @@
     token_rows = inputs[0]
     grad_rows = output_grad[0]
     gate_full, cand_full, out_full = (
-        lax.all_gather(w_gate, "seq", axis=0, tiled=True),
+        jnp.concatenate(
+            lax.all_to_all(jnp.stack([w_gate] * lax.axis_size("seq")), "seq", 0, 0), axis=0
+        ),
         lax.all_gather(w_cand, "seq", axis=0, tiled=True),
         lax.all_gather(w_out, "seq", axis=0, tiled=True),
     )

time: 1310 us -> 1060 us (0.81)
  waiting for transfers between devices: 1090 us -> 822 us
    all_gather x1 -> x0, waiting for transfers between devices: 344 us -> none  [on_device(): lax.all_gather(w_gate, 'seq', axis=0, tiled=True)]
    all_gather x1, waiting for transfers between devices: 362 us -> 427 us  [on_device(): lax.all_gather(w_cand, 'seq', axis=0, tiled=True)]
  transfers between devices with their start and end apart: 9 -> 9, of which waited for: 6 -> 6; matrix products, arithmetic and copies ran while one was open for 4% -> 5% of each run, Pallas kernels for 0% -> 0%
where the time goes in v1:
time: 1060 us; the launch traced here: 1050 us
  waiting for transfers between devices  822 us (78%)
  starting transfers between devices  63.3 us (6%)
  other arithmetic  56.4 us (5%)
  local copies, waits for them, and re-layouts  40.4 us (4%)
  matrix products  38.6 us (4%)
  blocking collectives  16.3 us (2%)
  between operations  15.2 us (1%)
    all_gather x1, waiting for transfers between devices, on_device(): lax.all_gather(w_cand, 'seq', axis=0, tiled=True)  427 us
    all_gather x1, waiting for transfers between devices, on_device(): lax.all_gather(w_out, 'seq', axis=0, tiled=True)  348 us
    add x25, other arithmetic, shift_scan(): drive = keep * drive_far + drive  40.4 us
  transfers between devices with their start and end apart: 9, of which 6 were waited for; matrix products, arithmetic and copies ran while one was open for 5% of the time, Pallas kernels for 0%

profile of v1, /device:TPU:8, one launch (start us, length us, event | category | flops | bytes accessed | tf_op | source)
XLA Modules:
  0.0 1052.6 jit_solution(13215187332507321735)
XLA Ops:
  7.9 5.2 stack.2
  13.1 12.3 %all-to-all-start = ((bf16[64,32,2048]{2,1,0:T(8,128)(2,1)}), bf16[64,32,2048]{2,1,0:T(8,128)(2,1)}, u32[]{:S(2)}, u32[]{:S(2)}) async-start(bf16[64,32,2048]{2,1,0:T(8,128)(2,1)} %stack.2), calls=%async_computation | async-start | bytes 16777216 | tf_op jit(solution)/shard_map/all_to_all | solution.py:38
  26.5 426.6 %all-gather.3.cloned.1.call-done = bf16[2048,2048]{1,0:T(8,128)(2,1)} async-done(((bf16[32,2048]{1,0:T(8,128)(2,1)}), bf16[2048,2048]{1,0:T(8,128)(2,1)}) %all-gather.3.cloned.1.call-update) | async-done | bytes 8388624 | tf_op jit(solution)/shard_map/all_gather | solution.py:40
  453.2 5.8 fusion.9
  460.3 9.9 all-to-all-start.2
  470.1 348.4 %all-gather.5.cloned.1.call-done = bf16[2048,2048]{1,0:T(8,128)(2,1)} async-done(((bf16[32,2048]{1,0:T(8,128)(2,1)}), bf16[2048,2048]{1,0:T(8,128)(2,1)}) %all-gather.5.cloned.1.call-update) | async-done | bytes 8388624 | tf_op jit(solution)/shard_map/all_gather | solution.py:41
  818.5 6.7 convolution_convert_fusion
  825.3 11.0 %all-to-all-start.4 = ((bf16[64,32,256]{2,1,0:T(8,128)(2,1)}), bf16[64,32,256]{2,1,0:T(8,128)(2,1)S(1)}, u32[]{:S(2)}, u32[]{:S(2)}) async-start(bf16[64,32,256]{2,1,0:T(8,128)(2,1)} %bitcast.140), calls=%async_computation.4 | async-start | bytes 2097152 | tf_op jit(solution)/shard_map/all_to_all | solution.py:73
  836.4 6.7 fusion.8
  843.1 2.3 copy.31
  845.4 9.1 all-to-all-done.4
  854.5 6.7 all-to-all-start.1
  866.3 12.9 %all-to-all-done.1 = bf16[64,32,256]{2,1,0:T(8,128)(2,1)} async-done(((bf16[64,32,256]{2,1,0:T(8,128)(2,1)}), bf16[64,32,256]{2,1,0:T(8,128)(2,1)}, u32[]{:S(2)}, u32[]{:S(2)}) %all-to-all-start.1) | async-done | bytes 1048608 | tf_op jit(solution)/shard_map/all_to_all | solution.py:60
  880.9 2.1 copy-done.8
  884.3 2.6 fusion.37
  888.9 4.3 multiply_add_fusion.27
  895.8 2.5 slice_multiply_fusion
  899.3 2.1 slice.296
  901.4 10.3 multiply_add_fusion.11
  911.7 4.6 multiply_add_fusion.25
  921.1 9.4 multiply_add_fusion.20
  950.3 2.8 fusion.34
  954.2 6.2 all-to-all-start.5
  960.4 2.8 multiply_convert_fusion
  964.5 14.2 %all-to-all-done.5 = bf16[32,64,256]{2,0,1:T(8,128)(2,1)} async-done(((bf16[32,64,256]{2,0,1:T(8,128)(2,1)}), bf16[32,64,256]{2,0,1:T(8,128)(2,1)}, u32[]{:S(2)}, u32[]{:S(2)}) %all-to-all-start.5) | async-done | bytes 1048608 | tf_op jit(solution)/shard_map/all_to_all | solution.py:84
  978.6 6.2 all-to-all-start.6
  986.0 16.3 %psum.7 = f32[32]{0:T(128)} all-reduce(f32[32]{0:T(128)S(1)} %get-tuple-element.16), channel_id=1, replica_groups=mesh['seq'=64,'batch'=4] {'batch'}, use_global_device_ids=true, to_apply=%region_4.0 | all-reduce | flops 32 | bytes 256 | tf_op jit(solution)/shard_map/psum | solution.py:108
  1003.6 10.8 %all-to-all-start.3 = ((bf16[32,64,256]{2,0,1:T(8,128)(2,1)}), bf16[32,64,256]{2,0,1:T(8,128)(2,1)S(1)}, u32[]{:S(2)}, u32[]{:S(2)}) async-start(bf16[32,64,256]{2,0,1:T(8,128)(2,1)} %bitcast.135), calls=%async_computation.3 | async-start | bytes 2097152 | tf_op jit(solution)/shard_map/all_to_all | solution.py:70
  1014.5 6.2 fusion.38
  1020.7 6.5 fusion.12
  1028.8 9.8 all-to-all-done.3
  1038.6 6.7 fusion.10
  (136 shorter events, 47.2 us)
Async XLA Ops:
  7.2 446.0 %all-gather.3.cloned.1.call-start = ((), (), s32[]{:S(2)}) async-start(), calls=%async_computation.7 | async-start | bytes 8519680 | tf_op jit(solution)/shard_map/all_gather | solution.py:40
  13.1 13.1 %copy-start.12 = (bf16[1,256,2048]{2,1,0:T(8,128)(2,1)S(1)}, bf16[1,256,2048]{2,1,0:T(8,128)(2,1)}, u32[]{:S(2)}) copy-start(bf16[1,256,2048]{2,1,0:T(8,128)(2,1)} %param.10) | copy-start | bytes 3145732
  13.1 440.0 %copy-start.23 = (f32[2048]{0:T(1024)S(1)}, f32[2048]{0:T(1024)}, u32[]{:S(2)}) copy-start(f32[2048]{0:T(1024)} %param.12) | copy-start | bytes 24580
  13.1 447.1 %all-to-all-start = ((bf16[64,32,2048]{2,1,0:T(8,128)(2,1)}), bf16[64,32,2048]{2,1,0:T(8,128)(2,1)}, u32[]{:S(2)}, u32[]{:S(2)}) async-start(bf16[64,32,2048]{2,1,0:T(8,128)(2,1)} %stack.2), calls=%async_computation | async-start | bytes 16777216 | tf_op jit(solution)/shard_map/all_to_all | solution.py:38
  25.5 793.1 %all-gather.5.cloned.1.call-start = ((), (), s32[]{:S(2)}) async-start(), calls=%async_computation.8 | async-start | bytes 8519680 | tf_op jit(solution)/shard_map/all_gather | solution.py:41
  26.5 809.8 %copy-start.20 = (f32[256]{0:T(256)}, f32[256]{0:T(256)S(1)}, u32[]{:S(2)}) copy-start(f32[256]{0:T(256)S(1)} %add_rsqrt_fusion) | copy-start | bytes 3076
  458.9 359.6 %copy-start.17 = (bf16[1,256,2048]{2,1,0:T(8,128)(2,1)S(1)}, bf16[1,256,2048]{2,1,0:T(8,128)(2,1)}, u32[]{:S(2)}) copy-start(bf16[1,256,2048]{2,1,0:T(8,128)(2,1)} %param.11) | copy-start | bytes 3145732
  460.3 365.0 %all-to-all-start.2 = ((bf16[64,32,256]{2,1,0:T(8,128)(2,1)}), bf16[64,32,256]{2,1,0:T(8,128)(2,1)S(1)}, u32[]{:S(2)}, u32[]{:S(2)}) async-start(bf16[64,32,256]{2,1,0:T(8,128)(2,1)} %bitcast.7), calls=%async_computation.2 | async-start | bytes 2097152 | tf_op jit(solution)/shard_map/all_to_all | solution.py:61
  825.3 29.2 %all-to-all-start.4 = ((bf16[64,32,256]{2,1,0:T(8,128)(2,1)}), bf16[64,32,256]{2,1,0:T(8,128)(2,1)S(1)}, u32[]{:S(2)}, u32[]{:S(2)}) async-start(bf16[64,32,256]{2,1,0:T(8,128)(2,1)} %bitcast.140), calls=%async_computation.4 | async-start | bytes 2097152 | tf_op jit(solution)/shard_map/all_to_all | solution.py:73
  843.1 18.1 %copy-start.22 = (f32[1,32]{1,0:T(1,128)S(1)}, f32[1,32]{1,0:T(1,128)}, u32[]{:S(2)}) copy-start(f32[1,32]{1,0:T(1,128)} %param.14) | copy-start | bytes 388
  854.5 6.8 copy-start.15
  854.5 24.7 %all-to-all-start.1 = ((bf16[64,32,256]{2,1,0:T(8,128)(2,1)}), bf16[64,32,256]{2,1,0:T(8,128)(2,1)}, u32[]{:S(2)}, u32[]{:S(2)}) async-start(bf16[64,32,256]{2,1,0:T(8,128)(2,1)} %bitcast.4), calls=%async_computation.1 | async-start | bytes 2097152 | tf_op jit(solution)/shard_map/all_to_all | solution.py:60
  864.2 2.1 copy-start.5
  880.7 2.4 copy-start.8
  880.7 2.3 copy-start.19
  880.9 3.3 copy-start.2
  884.2 2.6 copy-start.4
  888.9 4.3 copy-start
  893.2 1.6 copy-start.6
  893.2 2.2 copy-start.14
  895.4 3.5 copy-start.1
  899.3 2.1 copy-start.7
  933.9 1.6 copy-start.10
  948.1 1.6 copy-start.3
  948.1 2.2 copy-start.9
  954.2 24.5 %all-to-all-start.5 = ((bf16[32,64,256]{2,0,1:T(8,128)(2,1)}), bf16[32,64,256]{2,0,1:T(8,128)(2,1)}, u32[]{:S(2)}, u32[]{:S(2)}) async-start(bf16[32,64,256]{2,0,1:T(8,128)(2,1)} %bitcast.137), calls=%async_computation.5 | async-start | bytes 2097152 | tf_op jit(solution)/shard_map/all_to_all | solution.py:84
  978.6 25.0 %all-to-all-start.6 = ((bf16[32,64,256]{2,0,1:T(8,128)(2,1)}), bf16[32,64,256]{2,0,1:T(8,128)(2,1)}, u32[]{:S(2)}, u32[]{:S(2)}) async-start(bf16[32,64,256]{2,0,1:T(8,128)(2,1)} %bitcast.136), calls=%async_computation.6 | async-start | bytes 2097152 | tf_op jit(solution)/shard_map/all_to_all | solution.py:87
  1003.6 35.0 %all-to-all-start.3 = ((bf16[32,64,256]{2,0,1:T(8,128)(2,1)}), bf16[32,64,256]{2,0,1:T(8,128)(2,1)S(1)}, u32[]{:S(2)}, u32[]{:S(2)}) async-start(bf16[32,64,256]{2,0,1:T(8,128)(2,1)} %bitcast.135), calls=%async_computation.3 | async-start | bytes 2097152 | tf_op jit(solution)/shard_map/all_to_all | solution.py:70
  1014.4 6.2 copy-start.13
  1014.4 6.2 copy-start.21
  1014.5 6.2 copy-start.24
  1020.7 6.5 copy-start.18
  (2 other events, 3.1 us)
Sparse Core Ops, SparseCore 0:
  9.8 443.3 all-gather.2
  455.0 363.5 all-gather.4
